TPU v7x, 32 devices: a whole 2x2x4 slice. The times are simulated.
32 devices in a mesh: ka: 8 (over z, x), pt: 4 (over y, core).
Axes of the slice: x: 2, y: 2, z: 4, core: 2. Of those that a mesh axis runs over, the one named last changes fastest.
Arguments:
- wedge_orbitals: bfloat16 [2, 8, 4096, 128], P(None, 'ka', 'pt'), may hold values from -6 to 6
- star_members: int32 [8, 4], replicated, may hold values from -1 to 7, as said below
- star_ops: int32 [8, 4], replicated, may hold values from 0 to 47
- rotations: bfloat16 [48, 128, 128], replicated, may hold values from -0.5 to 0.5
- screen_left: bfloat16 [6, 4096, 64], P(None, 'pt'), may hold values from -2.5 to 2.5
- screen_right: bfloat16 [6, 4096, 64], P(None, 'pt'), may hold values from -2.5 to 2.5
Outputs:
- exchange_matrix: float32 [2, 8, 128, 128], P(None, 'ka', 'pt')
Inputs may be any that keep to these rules, and one draw needn't show every extreme that they name: `star_members`: every k-point 0 to 7 stands exactly once in the table; -1 marks an empty slot; the star of some wedge point fills all 4 slots.
All inputs are finite; a program needn't handle non-finite values.
Results may differ from a plain program's by a relative error of at most 0.0064.
Values may be sent and summed in bfloat16 or wider, within the bound.
No kernel may reach another device: no remote copies, remote signals or barrier semaphores. Data moves between devices by JAX's collectives and lax.ppermute only.
A program may use at most 128 MiB of HBM per device.

v0:
```python
import math
import jax
import jax.numpy as jnp
from jax import lax
from jax.sharding import PartitionSpec as P

NB = 128
NPTS = 4096
STOPS = 6
QBLK = 1024


def from_behind(block, axis, distance):
    devices = range(lax.axis_size(axis))
    route = [((i - distance) % len(devices), i) for i in devices]
    return lax.ppermute(block, axis, route)


def density_term(row_block, full_block, upper_half, lower_half, left_screen, right_screen):
    n_rows = row_block.shape[1]
    n_bands = row_block.shape[2]
    n_points = full_block.shape[1]
    left_rows = jnp.concatenate([row_block[0], row_block[1]], axis=1)
    swapped = jnp.concatenate([row_block[1], -row_block[0]], axis=1)
    stacked = jnp.concatenate([left_rows, swapped], axis=0)
    accum = jnp.zeros((n_rows, 2 * n_bands), jnp.float32)
    for column_block in range(n_points // QBLK):
        col_start = column_block * QBLK
        col_end = col_start + QBLK
        column_rows = jnp.concatenate(
            [full_block[0, col_start:col_end], full_block[1, col_start:col_end]], axis=1
        )
        density = lax.dot_general(
            stacked, column_rows, (((1,), (1,)), ((), ())), preferred_element_type=jnp.float32
        )
        screen_tile = lax.dot_general(
            left_screen,
            right_screen[col_start:col_end],
            (((1,), (1,)), ((), ())),
            preferred_element_type=jnp.float32,
        )
        real_part = (density[:n_rows] * screen_tile).astype(jnp.bfloat16)
        imag_part = (density[n_rows:] * screen_tile).astype(jnp.bfloat16)
        screened = jnp.concatenate([real_part, imag_part], axis=1)
        operand = jnp.concatenate(
            [upper_half[col_start:col_end], lower_half[col_start:col_end]], axis=0
        )
        accum = accum + jnp.dot(screened, operand, preferred_element_type=jnp.float32)
    return accum


def rotate_block(arrived, rotations, my_op):
    p_rows = arrived.shape[1]
    n_bands = arrived.shape[2]
    rotation = lax.dynamic_index_in_dim(rotations, my_op, 0, keepdims=False)
    product = jnp.dot(
        arrived.reshape(2 * p_rows, n_bands), rotation, preferred_element_type=jnp.float32
    )
    return product.astype(jnp.bfloat16).reshape(2, p_rows, n_bands)


def body(wedge_orbitals, star_members, star_ops, rotations, screen_left, screen_right):
    n_kpoints = lax.axis_size("ka")
    own_kpoint = lax.axis_index("ka")
    own_block = wedge_orbitals[:, 0]
    n_bands = own_block.shape[2]
    wedge_iota = jnp.arange(star_members.shape[0], dtype=jnp.int32)[:, None]
    located = star_members == own_kpoint
    wedge_source = jnp.sum(jnp.where(located, wedge_iota, 0))
    my_op = jnp.sum(jnp.where(located, star_ops, 0))
    my_star = lax.dynamic_index_in_dim(star_members, own_kpoint, 0, keepdims=False)
    target_iota = jnp.arange(n_kpoints, dtype=jnp.int32)
    wanted = jnp.any(my_star[None, :] == target_iota[:, None], axis=1)
    outgoing = jnp.where(
        wanted[:, None, None, None], own_block[None], jnp.zeros_like(own_block)[None]
    )
    incoming = lax.all_to_all(outgoing, "ka", split_axis=0, concat_axis=0, tiled=True)
    arrived = lax.dynamic_index_in_dim(incoming, wedge_source, 0, keepdims=False)
    rotated = rotate_block(arrived, rotations, my_op)
    full_block, right_all = (
        lax.all_gather(rotated, "pt", axis=1, tiled=True),
        lax.all_gather(screen_right, "pt", axis=1, tiled=True),
    )
    upper_half = jnp.concatenate([full_block[0], full_block[1]], axis=1)
    lower_half = jnp.concatenate([-full_block[1], full_block[0]], axis=1)
    lead_stops = STOPS // 2

    def stop_term(row_block, visited, stop):
        return density_term(
            row_block, visited, upper_half, lower_half, screen_left[stop], right_all[stop]
        )

    def gathered_rows(slice_rows):
        return lax.all_gather(slice_rows, "pt", axis=1, tiled=True)

    accum = stop_term(rotated, full_block, lead_stops)
    downward = rotated
    for stop in range(lead_stops + 1, STOPS):
        downward = from_behind(downward, "ka", 1)
        accum = accum + stop_term(downward, gathered_rows(downward), stop)
    upward = rotated
    for stop in range(lead_stops - 1, -1, -1):
        upward = from_behind(upward, "ka", -1)
        accum = accum + stop_term(upward, gathered_rows(upward), stop)
    rounded_y = accum.astype(jnp.bfloat16)
    y_real = rounded_y[:, :n_bands]
    y_imag = rounded_y[:, n_bands:]
    stacked_x = jnp.concatenate([rotated[0], rotated[1]], axis=0)
    right_stack = jnp.concatenate([rounded_y, jnp.concatenate([y_imag, -y_real], axis=1)], axis=0)
    partial_value = lax.dot_general(
        stacked_x, right_stack, (((0,), (0,)), ((), ())), preferred_element_type=jnp.float32
    )
    rows_out = n_bands // lax.axis_size("pt")
    summed = lax.psum(partial_value, "pt")
    kept = lax.dynamic_slice_in_dim(summed, lax.axis_index("pt") * rows_out, rows_out, 0)
    scale_factor = 1.0 / (4.0 * NPTS * math.sqrt(NB))
    kept = kept * scale_factor
    return jnp.stack([kept[:, :n_bands], kept[:, n_bands:]])[:, None]


def solution(mesh):
    return jax.shard_map(
        body,
        mesh=mesh,
        in_specs=(
            P(None, "ka", "pt", None),
            P(),
            P(),
            P(),
            P(None, "pt", None),
            P(None, "pt", None),
        ),
        out_specs=P(None, "ka", "pt", None),
        check_vma=False,
    )
```

profile of v0, /device:TPU:0, one launch (start us, length us, event | category | flops | bytes accessed | tf_op | source)
XLA Modules:
  0.0 436.4 jit_solution(8135102432398648651)
XLA Ops:
  11.1 7.4 %all-to-all-start = ((bf16[8,2,1024,128]{3,2,1,0:T(8,128)(2,1)}), bf16[8,2,1024,128]{3,2,1,0:T(8,128)(2,1)}, u32[]{:S(2)}, u32[]{:S(2)}) async-start(bf16[8,2,1024,128]{3,2,1,0:T(8,128)(2,1)} %broadcast_select_fusion), calls=%async_computation | async-start | bytes 8388608 | tf_op jit(solution)/shard_map/all_to_all | solution.py:77
  23.3 88.6 %all-to-all-done = bf16[8,2,1024,128]{3,2,1,0:T(8,128)(2,1)} async-done(((bf16[8,2,1024,128]{3,2,1,0:T(8,128)(2,1)}), bf16[8,2,1024,128]{3,2,1,0:T(8,128)(2,1)}, u32[]{:S(2)}, u32[]{:S(2)}) %all-to-all-start) | async-done | bytes 4194336 | tf_op jit(solution)/shard_map/all_to_all | solution.py:77
  116.4 14.0 %collective-permute-done = bf16[2,1024,128]{2,1,0:T(8,128)(2,1)S(1)} collective-permute-done((bf16[2,1024,128]{2,1,0:T(8,128)(2,1)}, bf16[2,1024,128]{2,1,0:T(8,128)(2,1)S(1)}, u32[]{:S(2)}, u32[]{:S(2)}) %collective-permute-start) | collective-permute-done | bytes 524320 | tf_op jit(solution)/shard_map/ppermute | solution.py:16
  132.2 11.0 %collective-permute-done.2 = bf16[2,1024,128]{2,1,0:T(8,128)(2,1)S(1)} collective-permute-done((bf16[2,1024,128]{2,1,0:T(8,128)(2,1)}, bf16[2,1024,128]{2,1,0:T(8,128)(2,1)S(1)}, u32[]{:S(2)}, u32[]{:S(2)}) %collective-permute-start.2) | collective-permute-done | bytes 524320 | tf_op jit(solution)/shard_map/ppermute | solution.py:16
  144.7 15.2 %collective-permute-done.1 = bf16[2,1024,128]{2,1,0:T(8,128)(2,1)S(1)} collective-permute-done((bf16[2,1024,128]{2,1,0:T(8,128)(2,1)}, bf16[2,1024,128]{2,1,0:T(8,128)(2,1)S(1)}, u32[]{:S(2)}, u32[]{:S(2)}) %collective-permute-start.1) | collective-permute-done | bytes 524320 | tf_op jit(solution)/shard_map/ppermute | solution.py:16
  162.6 10.1 %collective-permute-done.3 = bf16[2,1024,128]{2,1,0:T(8,128)(2,1)S(1)} collective-permute-done((bf16[2,1024,128]{2,1,0:T(8,128)(2,1)}, bf16[2,1024,128]{2,1,0:T(8,128)(2,1)S(1)}, u32[]{:S(2)}, u32[]{:S(2)}) %collective-permute-start.3) | collective-permute-done | bytes 524320 | tf_op jit(solution)/shard_map/ppermute | solution.py:16
  182.4 6.4 %collective-permute-done.4 = bf16[2,1024,128]{2,1,0:T(8,128)(2,1)S(1)} collective-permute-done((bf16[2,1024,128]{2,1,0:T(8,128)(2,1)S(1)}, bf16[2,1024,128]{2,1,0:T(8,128)(2,1)S(1)}, u32[]{:S(2)}, u32[]{:S(2)}) %collective-permute-start.4) | collective-permute-done | bytes 524320 | tf_op jit(solution)/shard_map/ppermute | solution.py:16
  196.5 4.7 %fusion.232 = f32[2048,1024]{0,1:T(8,128)} fusion(bf16[1024,128]{1,0:T(8,128)(2,1)S(1)} %get-tuple-element.101, bf16[1024,128]{1,0:T(8,128)(2,1)S(1)} %get-tuple-element.102, bf16[1024,128]{1,0:T(8,128)(2,1)S(1)} %get-tuple-element.127, bf16[1024,128]{1,0:T(8,128)(2,1)S(1)} %get-tuple-element.128, bf16[1024,128]{1,0:T(8,128)(2,1)S(1)} %get-tuple-element.126), kind=kOutput, calls=%fused_computation.259 | convolution fusion | flops 1078984704 | bytes 9699328 | tf_op jit(solution)/shard_map/dot_general | solution.py:33
  201.1 4.6 %fusion.236 = f32[2048,1024]{0,1:T(8,128)} fusion(bf16[1024,128]{1,0:T(8,128)(2,1)S(1)} %get-tuple-element.99, bf16[1024,128]{1,0:T(8,128)(2,1)S(1)} %get-tuple-element.100, bf16[1024,128]{1,0:T(8,128)(2,1)S(1)} %get-tuple-element.127, bf16[1024,128]{1,0:T(8,128)(2,1)S(1)} %get-tuple-element.128, bf16[1024,128]{1,0:T(8,128)(2,1)S(1)} %get-tuple-element.126), kind=kOutput, calls=%fused_computation.263 | convolution fusion | flops 1078984704 | bytes 9699328 | tf_op jit(solution)/shard_map/dot_general | solution.py:33
  205.7 4.7 %fusion.240 = f32[2048,1024]{0,1:T(8,128)} fusion(bf16[1024,128]{1,0:T(8,128)(2,1)S(1)} %get-tuple-element.97, bf16[1024,128]{1,0:T(8,128)(2,1)S(1)} %get-tuple-element.98, bf16[1024,128]{1,0:T(8,128)(2,1)S(1)} %get-tuple-element.127, bf16[1024,128]{1,0:T(8,128)(2,1)S(1)} %get-tuple-element.128, bf16[1024,128]{1,0:T(8,128)(2,1)S(1)} %get-tuple-element.126), kind=kOutput, calls=%fused_computation.267 | convolution fusion | flops 1078984704 | bytes 9699328 | tf_op jit(solution)/shard_map/dot_general | solution.py:33
  210.4 4.6 %fusion.244 = f32[2048,1024]{0,1:T(8,128)} fusion(bf16[1024,128]{1,0:T(8,128)(2,1)S(1)} %get-tuple-element.96, bf16[1024,128]{1,0:T(8,128)(2,1)S(1)} %get-tuple-element.95, bf16[1024,128]{1,0:T(8,128)(2,1)S(1)} %get-tuple-element.127, bf16[1024,128]{1,0:T(8,128)(2,1)S(1)} %get-tuple-element.128, bf16[1024,128]{1,0:T(8,128)(2,1)S(1)} %get-tuple-element.126), kind=kOutput, calls=%fused_computation.271 | convolution fusion | flops 1078984704 | bytes 9699328 | tf_op jit(solution)/shard_map/dot_general | solution.py:33
  215.0 4.4 %fusion.47 = (bf16[1024,1024]{0,1:T(8,128)(2,1)S(1)}, bf16[1024,1024]{0,1:T(8,128)(2,1)S(1)}) fusion(f32[2048,1024]{0,1:T(8,128)} %fusion.232, bf16[6,4096,64]{1,2,0:T(8,128)(2,1)} %all-gather.10.cloned.1.call-done, bf16[6,1024,64]{1,2,0:T(8,128)(2,1)S(1)} %copy-done.3), kind=kOutput, calls=%fused_computation.95 | convolution fusion | flops 138412032 | bytes 12845056 | tf_op jit(solution)/shard_map/dot_general | solution.py:36
  241.9 4.7 %fusion.252 = f32[2048,1024]{0,1:T(8,128)} fusion(bf16[1024,128]{1,0:T(8,128)(2,1)S(1)} %get-tuple-element.91, bf16[1024,128]{1,0:T(8,128)(2,1)S(1)} %get-tuple-element.92, bf16[1024,128]{1,0:T(8,128)(2,1)S(1)} %fusion.453, bf16[1024,128]{1,0:T(8,128)(2,1)S(1)} %copy-done.14, bf16[1024,128]{1,0:T(8,128)(2,1)S(1)} %copy-done.13), kind=kOutput, calls=%fused_computation.279 | convolution fusion | flops 1078984704 | bytes 9699328 | tf_op jit(solution)/shard_map/dot_general | solution.py:33
  246.6 4.6 %fusion.256 = f32[2048,1024]{0,1:T(8,128)} fusion(bf16[1024,128]{1,0:T(8,128)(2,1)S(1)} %get-tuple-element.89, bf16[1024,128]{1,0:T(8,128)(2,1)S(1)} %get-tuple-element.90, bf16[1024,128]{1,0:T(8,128)(2,1)S(1)} %fusion.453, bf16[1024,128]{1,0:T(8,128)(2,1)S(1)} %copy-done.14, bf16[1024,128]{1,0:T(8,128)(2,1)S(1)} %copy-done.13), kind=kOutput, calls=%fused_computation.283 | convolution fusion | flops 1078984704 | bytes 9699328 | tf_op jit(solution)/shard_map/dot_general | solution.py:33
  251.2 4.7 %fusion.260 = f32[2048,1024]{0,1:T(8,128)} fusion(bf16[1024,128]{1,0:T(8,128)(2,1)S(1)} %get-tuple-element.88, bf16[1024,128]{1,0:T(8,128)(2,1)S(1)} %get-tuple-element.87, bf16[1024,128]{1,0:T(8,128)(2,1)S(1)} %fusion.453, bf16[1024,128]{1,0:T(8,128)(2,1)S(1)} %copy-done.14, bf16[1024,128]{1,0:T(8,128)(2,1)S(1)} %copy-done.13), kind=kOutput, calls=%fused_computation.287 | convolution fusion | flops 1078984704 | bytes 9699328 | tf_op jit(solution)/shard_map/dot_general | solution.py:33
  272.1 5.2 %fusion.203 = f32[1024,256]{1,0:T(8,128)} fusion(f32[1024,256]{1,0:T(8,128)} %fusion.64, bf16[1024,1024]{0,1:T(8,128)(2,1)} %get-tuple-element.44, bf16[1024,1024]{0,1:T(8,128)(2,1)} %get-tuple-element.43, bf16[1024,256]{1,0:T(8,128)(2,1)} %get-tuple-element.111, bf16[1024,256]{1,0:T(8,128)(2,1)} %get-tuple-element.105), kind=kOutput, calls=%fused_computation.228 | convolution fusion | flops 1084489728 | bytes 7340032 | tf_op jit(solution)/shard_map/dot_general | solution.py:48
  304.5 4.6 %fusion.268 = f32[2048,1024]{0,1:T(8,128)} fusion(bf16[1024,128]{1,0:T(8,128)(2,1)S(1)} %get-tuple-element.83, bf16[1024,128]{1,0:T(8,128)(2,1)S(1)} %get-tuple-element.84, bf16[1024,128]{1,0:T(8,128)(2,1)S(1)} %fusion.454, bf16[1024,128]{1,0:T(8,128)(2,1)S(1)} %copy-done.9, bf16[1024,128]{1,0:T(8,128)(2,1)S(1)} %copy-done.8), kind=kOutput, calls=%fused_computation.295 | convolution fusion | flops 1078984704 | bytes 9699328 | tf_op jit(solution)/shard_map/dot_general | solution.py:33
  309.1 4.7 %fusion.272 = f32[2048,1024]{0,1:T(8,128)} fusion(bf16[1024,128]{1,0:T(8,128)(2,1)S(1)} %get-tuple-element.81, bf16[1024,128]{1,0:T(8,128)(2,1)S(1)} %get-tuple-element.82, bf16[1024,128]{1,0:T(8,128)(2,1)S(1)} %fusion.454, bf16[1024,128]{1,0:T(8,128)(2,1)S(1)} %copy-done.9, bf16[1024,128]{1,0:T(8,128)(2,1)S(1)} %copy-done.8), kind=kOutput, calls=%fused_computation.299 | convolution fusion | flops 1078984704 | bytes 9699328 | tf_op jit(solution)/shard_map/dot_general | solution.py:33
  313.8 4.6 %fusion.276 = f32[2048,1024]{0,1:T(8,128)} fusion(bf16[1024,128]{1,0:T(8,128)(2,1)S(1)} %get-tuple-element.80, bf16[1024,128]{1,0:T(8,128)(2,1)S(1)} %get-tuple-element.79, bf16[1024,128]{1,0:T(8,128)(2,1)S(1)} %fusion.454, bf16[1024,128]{1,0:T(8,128)(2,1)S(1)} %copy-done.9, bf16[1024,128]{1,0:T(8,128)(2,1)S(1)} %copy-done.8), kind=kOutput, calls=%fused_computation.303 | convolution fusion | flops 1078984704 | bytes 9699328 | tf_op jit(solution)/shard_map/dot_general | solution.py:33
  320.1 4.7 %fusion.296 = f32[2048,1024]{0,1:T(8,128)} fusion(bf16[1024,128]{1,0:T(8,128)(2,1)S(1)} %get-tuple-element.69, bf16[1024,128]{1,0:T(8,128)(2,1)S(1)} %get-tuple-element.70, bf16[1024,128]{1,0:T(8,128)(2,1)S(1)} %fusion.456, bf16[1024,128]{1,0:T(8,128)(2,1)S(1)} %copy-done.7, bf16[1024,128]{1,0:T(8,128)(2,1)S(1)} %get-tuple-element.118), kind=kOutput, calls=%fused_computation.323 | convolution fusion | flops 1078984704 | bytes 9699328 | tf_op jit(solution)/shard_map/dot_general | solution.py:33
  324.8 4.7 %fusion.300 = f32[2048,1024]{0,1:T(8,128)} fusion(bf16[1024,128]{1,0:T(8,128)(2,1)S(1)} %get-tuple-element.67, bf16[1024,128]{1,0:T(8,128)(2,1)S(1)} %get-tuple-element.68, bf16[1024,128]{1,0:T(8,128)(2,1)S(1)} %fusion.456, bf16[1024,128]{1,0:T(8,128)(2,1)S(1)} %copy-done.7, bf16[1024,128]{1,0:T(8,128)(2,1)S(1)} %get-tuple-element.118), kind=kOutput, calls=%fused_computation.327 | convolution fusion | flops 1078984704 | bytes 9699328 | tf_op jit(solution)/shard_map/dot_general | solution.py:33
  337.2 5.2 %fusion.191 = f32[1024,256]{1,0:T(8,128)} fusion(f32[1024,256]{1,0:T(8,128)} %fusion.80, bf16[1024,1024]{0,1:T(8,128)(2,1)} %get-tuple-element.36, bf16[1024,1024]{0,1:T(8,128)(2,1)} %get-tuple-element.35, bf16[1024,256]{1,0:T(8,128)(2,1)} %get-tuple-element.111, bf16[1024,256]{1,0:T(8,128)(2,1)} %get-tuple-element.105), kind=kOutput, calls=%fused_computation.224 | convolution fusion | flops 1084489728 | bytes 7340032 | tf_op jit(solution)/shard_map/dot_general | solution.py:48
  345.9 6.4 %fusion.15 = (bf16[1024,1024]{0,1:T(8,128)(2,1)}, bf16[1024,1024]{0,1:T(8,128)(2,1)}) fusion(f32[2048,1024]{0,1:T(8,128)} %fusion.296, bf16[6,4096,64]{1,2,0:T(8,128)(2,1)} %all-gather.10.cloned.1.call-done, bf16[6,1024,64]{1,2,0:T(8,128)(2,1)S(1)} %copy-done.3), kind=kOutput, calls=%fused_computation.31 | convolution fusion | flops 138412032 | bytes 12845056 | tf_op jit(solution)/shard_map/dot_general | solution.py:36
  394.0 33.9 %all-reduce.2.cloned.1.call-done = f32[128,256]{1,0:T(8,128)} async-done(((f32[128,256]{1,0:T(8,128)}), f32[128,256]{1,0:T(8,128)}) %all-reduce.2.cloned.1.call-update) | async-done | bytes 131088 | tf_op jit(solution)/shard_map/psum | solution.py:114
  (308 shorter events, 153.8 us)
Async XLA Ops:
  6.5 106.4 %copy-start = (bf16[48,128,128]{2,1,0:T(8,128)(2,1)S(1)}, bf16[48,128,128]{2,1,0:T(8,128)(2,1)}, u32[]{:S(2)}) copy-start(bf16[48,128,128]{2,1,0:T(8,128)(2,1)} %param.9) | copy-start | bytes 4718596
  11.1 7.5 %copy-start.64 = (s32[8,4]{0,1:T(4,128)S(1)}, s32[8,4]{0,1:T(4,128)}, u32[]{:S(2)}) copy-start(s32[8,4]{0,1:T(4,128)} %param.8) | copy-start | bytes 388
  11.1 100.7 %all-to-all-start = ((bf16[8,2,1024,128]{3,2,1,0:T(8,128)(2,1)}), bf16[8,2,1024,128]{3,2,1,0:T(8,128)(2,1)}, u32[]{:S(2)}, u32[]{:S(2)}) async-start(bf16[8,2,1024,128]{3,2,1,0:T(8,128)(2,1)} %broadcast_select_fusion), calls=%async_computation | async-start | bytes 8388608 | tf_op jit(solution)/shard_map/all_to_all | solution.py:77
  18.6 172.0 %all-gather.8.cloned.1.call-start = ((), (), s32[]{:S(2)}) async-start(), calls=%async_computation.1 | async-start | bytes 2621440 | tf_op jit(solution)/shard_map/all_gather | solution.py:81
  114.0 59.6 %copy-start.15 = (bf16[2048,128]{1,0:T(8,128)(2,1)S(1)}, bf16[2048,128]{1,0:T(8,128)(2,1)}, u32[]{:S(2)}) copy-start(bf16[2048,128]{1,0:T(8,128)(2,1)} %convolution_convert_fusion) | copy-start | bytes 1572868
  114.1 100.9 %all-gather.10.cloned.1.call-start = ((), (), s32[]{:S(2)}) async-start(), calls=%async_computation.2 | async-start | bytes 3932160 | tf_op jit(solution)/shard_map/all_gather | solution.py:82
  114.8 120.0 %all-gather.12.cloned.1.call-start = ((), (), s32[]{:S(2)}) async-start(), calls=%async_computation.3 | async-start | bytes 2621440 | tf_op jit(solution)/shard_map/all_gather | solution.py:94
  114.9 15.5 %collective-permute-start = (bf16[2,1024,128]{2,1,0:T(8,128)(2,1)}, bf16[2,1024,128]{2,1,0:T(8,128)(2,1)S(1)}, u32[]{:S(2)}, u32[]{:S(2)}) collective-permute-start(bf16[2,1024,128]{2,1,0:T(8,128)(2,1)} %bitcast.397), channel_id=1, source_target_pairs={{28,0},{0,4},{4,8},{8,12},{12,16},{16,20},{20,24},{24,28},{29,1},{... | collective-permute-start | bytes 1572872 | tf_op jit(solution)/shard_map/ppermute | solution.py:16
  131.2 42.5 %copy-start.25 = (bf16[2,1024,128]{2,1,0:T(8,128)(2,1)S(1)}, bf16[2,1024,128]{2,1,0:T(8,128)(2,1)}, u32[]{:S(2)}) copy-start(bf16[2,1024,128]{2,1,0:T(8,128)(2,1)} %copy-done.24) | copy-start | bytes 1572868
  131.2 124.6 %all-gather.16.cloned.1.call-start = ((), (), s32[]{:S(2)}) async-start(), calls=%async_computation.5 | async-start | bytes 2621440 | tf_op jit(solution)/shard_map/all_gather | solution.py:94
  131.3 12.0 %collective-permute-start.2 = (bf16[2,1024,128]{2,1,0:T(8,128)(2,1)}, bf16[2,1024,128]{2,1,0:T(8,128)(2,1)S(1)}, u32[]{:S(2)}, u32[]{:S(2)}) collective-permute-start(bf16[2,1024,128]{2,1,0:T(8,128)(2,1)} %bitcast.398), channel_id=1, source_target_pairs={{4,0},{8,4},{12,8},{16,12},{20,16},{24,20},{28,24},{0,28},{5,1},{9... | collective-permute-start | bytes 1572872 | tf_op jit(solution)/shard_map/ppermute | solution.py:16
  144.1 29.7 %copy-start.23 = (bf16[2,1024,128]{2,1,0:T(8,128)(2,1)S(1)}, bf16[2,1024,128]{2,1,0:T(8,128)(2,1)}, u32[]{:S(2)}) copy-start(bf16[2,1024,128]{2,1,0:T(8,128)(2,1)} %copy-done.22) | copy-start | bytes 1572868
  144.1 153.3 %all-gather.14.cloned.1.call-start = ((), (), s32[]{:S(2)}) async-start(), calls=%async_computation.4 | async-start | bytes 2621440 | tf_op jit(solution)/shard_map/all_gather | solution.py:94
  144.2 15.7 %collective-permute-start.1 = (bf16[2,1024,128]{2,1,0:T(8,128)(2,1)}, bf16[2,1024,128]{2,1,0:T(8,128)(2,1)S(1)}, u32[]{:S(2)}, u32[]{:S(2)}) collective-permute-start(bf16[2,1024,128]{2,1,0:T(8,128)(2,1)} %copy-done.24), channel_id=1, source_target_pairs={{28,0},{0,4},{4,8},{8,12},{12,16},{16,20},{20,24},{24,28},{29,1},{... | collective-permute-start | bytes 1572872 | tf_op jit(solution)/shard_map/ppermute | solution.py:16
  160.7 157.7 %all-gather.18.cloned.1.call-start = ((), (), s32[]{:S(2)}) async-start(), calls=%async_computation.6 | async-start | bytes 2621440 | tf_op jit(solution)/shard_map/all_gather | solution.py:94
  160.8 11.9 %collective-permute-start.3 = (bf16[2,1024,128]{2,1,0:T(8,128)(2,1)}, bf16[2,1024,128]{2,1,0:T(8,128)(2,1)S(1)}, u32[]{:S(2)}, u32[]{:S(2)}) collective-permute-start(bf16[2,1024,128]{2,1,0:T(8,128)(2,1)} %copy-done.22), channel_id=1, source_target_pairs={{4,0},{8,4},{12,8},{16,12},{20,16},{24,20},{28,24},{0,28},{5,1},{9... | collective-permute-start | bytes 1572872 | tf_op jit(solution)/shard_map/ppermute | solution.py:16
  173.6 199.8 %all-gather.20.cloned.1.call-start = ((), (), s32[]{:S(2)}) async-start(), calls=%async_computation.7 | async-start | bytes 2621440 | tf_op jit(solution)/shard_map/all_gather | solution.py:94
  176.4 12.3 %collective-permute-start.4 = (bf16[2,1024,128]{2,1,0:T(8,128)(2,1)S(1)}, bf16[2,1024,128]{2,1,0:T(8,128)(2,1)S(1)}, u32[]{:S(2)}, u32[]{:S(2)}) collective-permute-start(bf16[2,1024,128]{2,1,0:T(8,128)(2,1)S(1)} %copy-done.19), channel_id=1, source_target_pairs={{4,0},{8,4},{12,8},{16,12},{20,16},{24,20},{28,24},{0,28},{5,1},{9... | collective-permute-start | bytes 1572872 | tf_op jit(solution)/shard_map/ppermute | solution.py:16
  190.4 237.4 %all-reduce.2.cloned.1.call-start = ((), (), s32[]{:S(2)}) async-start(), calls=%async_computation.8 | async-start | bytes 262144 | tf_op jit(solution)/shard_map/psum | solution.py:114
  268.2 9.1 %slice-start.2 = ((s8[8388608]{0:T(1024)(128)(4,1)}), s8[4194304]{0:T(1024)(128)(4,1)S(1)}, s32[]{:S(2)}) async-start(s8[8388608]{0:T(1024)(128)(4,1)} %bitcast.378), calls=%async_computation.11 | async-start | bytes 8388608
  333.2 9.2 %slice-start.6 = ((s8[8388608]{0:T(1024)(128)(4,1)}), s8[4194304]{0:T(1024)(128)(4,1)S(1)}, s32[]{:S(2)}) async-start(s8[8388608]{0:T(1024)(128)(4,1)} %bitcast.382), calls=%async_computation.15 | async-start | bytes 8388608
  333.2 10.8 %slice-start.8 = ((s8[8388608]{0:T(1024)(128)(4,1)}), s8[4194304]{0:T(1024)(128)(4,1)S(1)}, s32[]{:S(2)}) async-start(s8[8388608]{0:T(1024)(128)(4,1)} %bitcast.384), calls=%async_computation.17 | async-start | bytes 8388608
  344.1 8.2 %slice-start.14 = ((s8[8388608]{0:T(1024)(128)(4,1)}), s8[4194304]{0:T(1024)(128)(4,1)S(1)}, s32[]{:S(2)}) async-start(s8[8388608]{0:T(1024)(128)(4,1)} %bitcast.390), calls=%async_computation.23 | async-start | bytes 8388608
  391.5 37.7 %copy-start.1 = (bf16[48,128,128]{2,1,0:T(8,128)(2,1)S(1)}, bf16[48,128,128]{2,1,0:T(8,128)(2,1)}, u32[]{:S(2)}) copy-start(bf16[48,128,128]{2,1,0:T(8,128)(2,1)} %param.9) | copy-start | bytes 4718596
  (81 other events, 193.9 us)
Sparse Core Ops, SparseCore 0:
  114.2 21.6 all-gather.7
  137.4 28.4 all-gather.9
  167.5 22.5 all-gather.11
  191.5 22.5 all-gather.15
  215.5 22.5 all-gather.13
  239.6 22.5 all-gather.17
  263.7 22.5 all-gather.19
  394.1 33.7 all-reduce.1
where the time goes:
time: 440 us; the launch traced here: 436 us
  waiting for transfers between devices  180 us (41%)
  matrix products  179 us (41%)
  local copies, waits for them, and re-layouts  30.9 us (7%)
  between operations  19 us (4%)
  starting transfers between devices  16.8 us (4%)
  other arithmetic  10.3 us (2%)
    all_to_all x1, waiting for transfers between devices, body(): lax.all_to_all(outgoing, 'ka', split_axis=0, concat_axis=0, tiled=True)  88.6 us
    dot_general x24, matrix products, density_term(): lax.dot_general(stacked, column_rows, (((1,), (1,)), ((), ())), preferred...  71.7 us
    dot_general x24, matrix products, density_term(): lax.dot_general(left_screen, right_screen[col_start:col_end], (((1,), (1,...  57.9 us
    ppermute x5, waiting for transfers between devices, from_behind(): return lax.ppermute(block, axis, route)  56.7 us
    dot_general x24, matrix products, density_term(): jnp.dot(screened, operand, preferred_element_type=jnp.float32)  47.6 us
    psum x1, waiting for transfers between devices, body(): summed = lax.psum(partial_value, 'pt')  33.9 us
    unnamed x182, local copies, waits for them, and re-layouts  14.2 us
    ppermute x5, starting transfers between devices, from_behind(): return lax.ppermute(block, axis, route)  9.08 us
  transfers between devices with their start and end apart: 14, of which 7 were waited for; matrix products, arithmetic and copies ran while one was open for 41% of the time, Pallas kernels for 0%

commit v1 on v0

--- a/solution.py
+++ b/solution.py
@@ -111,7 +111,8 @@
         stacked_x, right_stack, (((0,), (0,)), ((), ())), preferred_element_type=jnp.float32
     )
     rows_out = n_bands // lax.axis_size("pt")
-    summed = lax.psum(partial_value, "pt")
+    terms = lax.all_gather(partial_value, "pt")
+    summed = jnp.sum(terms, axis=0)
     kept = lax.dynamic_slice_in_dim(summed, lax.axis_index("pt") * rows_out, rows_out, 0)
     scale_factor = 1.0 / (4.0 * NPTS * math.sqrt(NB))
     kept = kept * scale_factor

time: 440 us -> 412 us (0.936)
  waiting for transfers between devices: 180 us -> 147 us
  blocking collectives: 0 us -> 7.34 us
    psum x1 -> x0, waiting for transfers between devices: 33.9 us -> none  [body(): summed = lax.psum(partial_value, 'pt')]
    all_gather x0 -> x1, blocking collectives: none -> 7.34 us  [body(): terms = lax.all_gather(partial_value, 'pt')]
  transfers between devices with their start and end apart: 14 -> 13, of which waited for: 7 -> 6; matrix products, arithmetic and copies ran while one was open for 41% -> 44% of each run, Pallas kernels for 0% -> 0%
where the time goes in v1:
time: 412 us; the launch traced here: 408 us
  matrix products  179 us (43%)
  waiting for transfers between devices  147 us (36%)
  local copies, waits for them, and re-layouts  30.7 us (7%)
  between operations  18.7 us (5%)
  starting transfers between devices  16.8 us (4%)
  other arithmetic  9.58 us (2%)
  blocking collectives  7.34 us (2%)
    all_to_all x1, waiting for transfers between devices, body(): lax.all_to_all(outgoing, 'ka', split_axis=0, concat_axis=0, tiled=True)  89 us
    dot_general x24, matrix products, density_term(): lax.dot_general(stacked, column_rows, (((1,), (1,)), ((), ())), preferred...  71.6 us
    dot_general x24, matrix products, density_term(): lax.dot_general(left_screen, right_screen[col_start:col_end], (((1,), (1,...  57.9 us
    ppermute x5, waiting for transfers between devices, from_behind(): return lax.ppermute(block, axis, route)  56.8 us
    dot_general x24, matrix products, density_term(): jnp.dot(screened, operand, preferred_element_type=jnp.float32)  47.6 us
    unnamed x182, local copies, waits for them, and re-layouts  14.1 us
    ppermute x5, starting transfers between devices, from_behind(): return lax.ppermute(block, axis, route)  9.14 us
    squeeze x6, local copies, waits for them, and re-layouts, density_term(): full_block[0, col_start:col_end]  8.67 us
  transfers between devices with their start and end apart: 13, of which 6 were waited for; matrix products, arithmetic and copies ran while one was open for 44% of the time, Pallas kernels for 0%

profile of v1, /device:TPU:0, one launch (start us, length us, event | category | flops | bytes accessed | tf_op | source)
XLA Modules:
  0.0 408.3 jit_solution(12650494155937283890)
XLA Ops:
  11.1 7.4 %all-to-all-start = ((bf16[8,2,1024,128]{3,2,1,0:T(8,128)(2,1)}), bf16[8,2,1024,128]{3,2,1,0:T(8,128)(2,1)}, u32[]{:S(2)}, u32[]{:S(2)}) async-start(bf16[8,2,1024,128]{3,2,1,0:T(8,128)(2,1)} %broadcast_select_fusion), calls=%async_computation | async-start | bytes 8388608 | tf_op jit(solution)/shard_map/all_to_all | solution.py:77
  22.9 89.0 %all-to-all-done = bf16[8,2,1024,128]{3,2,1,0:T(8,128)(2,1)} async-done(((bf16[8,2,1024,128]{3,2,1,0:T(8,128)(2,1)}), bf16[8,2,1024,128]{3,2,1,0:T(8,128)(2,1)}, u32[]{:S(2)}, u32[]{:S(2)}) %all-to-all-start) | async-done | bytes 4194336 | tf_op jit(solution)/shard_map/all_to_all | solution.py:77
  116.4 14.0 %collective-permute-done = bf16[2,1024,128]{2,1,0:T(8,128)(2,1)S(1)} collective-permute-done((bf16[2,1024,128]{2,1,0:T(8,128)(2,1)}, bf16[2,1024,128]{2,1,0:T(8,128)(2,1)S(1)}, u32[]{:S(2)}, u32[]{:S(2)}) %collective-permute-start) | collective-permute-done | bytes 524320 | tf_op jit(solution)/shard_map/ppermute | solution.py:16
  132.2 11.0 %collective-permute-done.2 = bf16[2,1024,128]{2,1,0:T(8,128)(2,1)S(1)} collective-permute-done((bf16[2,1024,128]{2,1,0:T(8,128)(2,1)}, bf16[2,1024,128]{2,1,0:T(8,128)(2,1)S(1)}, u32[]{:S(2)}, u32[]{:S(2)}) %collective-permute-start.2) | collective-permute-done | bytes 524320 | tf_op jit(solution)/shard_map/ppermute | solution.py:16
  144.7 15.2 %collective-permute-done.1 = bf16[2,1024,128]{2,1,0:T(8,128)(2,1)S(1)} collective-permute-done((bf16[2,1024,128]{2,1,0:T(8,128)(2,1)}, bf16[2,1024,128]{2,1,0:T(8,128)(2,1)S(1)}, u32[]{:S(2)}, u32[]{:S(2)}) %collective-permute-start.1) | collective-permute-done | bytes 524320 | tf_op jit(solution)/shard_map/ppermute | solution.py:16
  162.6 10.1 %collective-permute-done.3 = bf16[2,1024,128]{2,1,0:T(8,128)(2,1)S(1)} collective-permute-done((bf16[2,1024,128]{2,1,0:T(8,128)(2,1)}, bf16[2,1024,128]{2,1,0:T(8,128)(2,1)S(1)}, u32[]{:S(2)}, u32[]{:S(2)}) %collective-permute-start.3) | collective-permute-done | bytes 524320 | tf_op jit(solution)/shard_map/ppermute | solution.py:16
  182.3 6.5 %collective-permute-done.4 = bf16[2,1024,128]{2,1,0:T(8,128)(2,1)S(1)} collective-permute-done((bf16[2,1024,128]{2,1,0:T(8,128)(2,1)S(1)}, bf16[2,1024,128]{2,1,0:T(8,128)(2,1)S(1)}, u32[]{:S(2)}, u32[]{:S(2)}) %collective-permute-start.4) | collective-permute-done | bytes 524320 | tf_op jit(solution)/shard_map/ppermute | solution.py:16
  196.3 4.7 %fusion.232 = f32[2048,1024]{0,1:T(8,128)} fusion(bf16[1024,128]{1,0:T(8,128)(2,1)S(1)} %get-tuple-element.101, bf16[1024,128]{1,0:T(8,128)(2,1)S(1)} %get-tuple-element.102, bf16[1024,128]{1,0:T(8,128)(2,1)S(1)} %get-tuple-element.127, bf16[1024,128]{1,0:T(8,128)(2,1)S(1)} %get-tuple-element.128, bf16[1024,128]{1,0:T(8,128)(2,1)S(1)} %get-tuple-element.126), kind=kOutput, calls=%fused_computation.259 | convolution fusion | flops 1078984704 | bytes 9699328 | tf_op jit(solution)/shard_map/dot_general | solution.py:33
  201.0 4.6 %fusion.236 = f32[2048,1024]{0,1:T(8,128)} fusion(bf16[1024,128]{1,0:T(8,128)(2,1)S(1)} %get-tuple-element.99, bf16[1024,128]{1,0:T(8,128)(2,1)S(1)} %get-tuple-element.100, bf16[1024,128]{1,0:T(8,128)(2,1)S(1)} %get-tuple-element.127, bf16[1024,128]{1,0:T(8,128)(2,1)S(1)} %get-tuple-element.128, bf16[1024,128]{1,0:T(8,128)(2,1)S(1)} %get-tuple-element.126), kind=kOutput, calls=%fused_computation.263 | convolution fusion | flops 1078984704 | bytes 9699328 | tf_op jit(solution)/shard_map/dot_general | solution.py:33
  205.6 4.7 %fusion.240 = f32[2048,1024]{0,1:T(8,128)} fusion(bf16[1024,128]{1,0:T(8,128)(2,1)S(1)} %get-tuple-element.97, bf16[1024,128]{1,0:T(8,128)(2,1)S(1)} %get-tuple-element.98, bf16[1024,128]{1,0:T(8,128)(2,1)S(1)} %get-tuple-element.127, bf16[1024,128]{1,0:T(8,128)(2,1)S(1)} %get-tuple-element.128, bf16[1024,128]{1,0:T(8,128)(2,1)S(1)} %get-tuple-element.126), kind=kOutput, calls=%fused_computation.267 | convolution fusion | flops 1078984704 | bytes 9699328 | tf_op jit(solution)/shard_map/dot_general | solution.py:33
  210.3 4.5 %fusion.244 = f32[2048,1024]{0,1:T(8,128)} fusion(bf16[1024,128]{1,0:T(8,128)(2,1)S(1)} %get-tuple-element.96, bf16[1024,128]{1,0:T(8,128)(2,1)S(1)} %get-tuple-element.95, bf16[1024,128]{1,0:T(8,128)(2,1)S(1)} %get-tuple-element.127, bf16[1024,128]{1,0:T(8,128)(2,1)S(1)} %get-tuple-element.128, bf16[1024,128]{1,0:T(8,128)(2,1)S(1)} %get-tuple-element.126), kind=kOutput, calls=%fused_computation.271 | convolution fusion | flops 1078984704 | bytes 9699328 | tf_op jit(solution)/shard_map/dot_general | solution.py:33
  214.9 4.4 %fusion.47 = (bf16[1024,1024]{0,1:T(8,128)(2,1)S(1)}, bf16[1024,1024]{0,1:T(8,128)(2,1)S(1)}) fusion(f32[2048,1024]{0,1:T(8,128)} %fusion.232, bf16[6,4096,64]{1,2,0:T(8,128)(2,1)} %all-gather.11.cloned.1.call-done, bf16[6,1024,64]{1,2,0:T(8,128)(2,1)S(1)} %copy-done.3), kind=kOutput, calls=%fused_computation.95 | convolution fusion | flops 138412032 | bytes 12845056 | tf_op jit(solution)/shard_map/dot_general | solution.py:36
  241.7 4.7 %fusion.252 = f32[2048,1024]{0,1:T(8,128)} fusion(bf16[1024,128]{1,0:T(8,128)(2,1)S(1)} %get-tuple-element.91, bf16[1024,128]{1,0:T(8,128)(2,1)S(1)} %get-tuple-element.92, bf16[1024,128]{1,0:T(8,128)(2,1)S(1)} %fusion.453, bf16[1024,128]{1,0:T(8,128)(2,1)S(1)} %copy-done.14, bf16[1024,128]{1,0:T(8,128)(2,1)S(1)} %copy-done.13), kind=kOutput, calls=%fused_computation.279 | convolution fusion | flops 1078984704 | bytes 9699328 | tf_op jit(solution)/shard_map/dot_general | solution.py:33
  246.4 4.6 %fusion.256 = f32[2048,1024]{0,1:T(8,128)} fusion(bf16[1024,128]{1,0:T(8,128)(2,1)S(1)} %get-tuple-element.89, bf16[1024,128]{1,0:T(8,128)(2,1)S(1)} %get-tuple-element.90, bf16[1024,128]{1,0:T(8,128)(2,1)S(1)} %fusion.453, bf16[1024,128]{1,0:T(8,128)(2,1)S(1)} %copy-done.14, bf16[1024,128]{1,0:T(8,128)(2,1)S(1)} %copy-done.13), kind=kOutput, calls=%fused_computation.283 | convolution fusion | flops 1078984704 | bytes 9699328 | tf_op jit(solution)/shard_map/dot_general | solution.py:33
  251.0 4.7 %fusion.260 = f32[2048,1024]{0,1:T(8,128)} fusion(bf16[1024,128]{1,0:T(8,128)(2,1)S(1)} %get-tuple-element.88, bf16[1024,128]{1,0:T(8,128)(2,1)S(1)} %get-tuple-element.87, bf16[1024,128]{1,0:T(8,128)(2,1)S(1)} %fusion.453, bf16[1024,128]{1,0:T(8,128)(2,1)S(1)} %copy-done.14, bf16[1024,128]{1,0:T(8,128)(2,1)S(1)} %copy-done.13), kind=kOutput, calls=%fused_computation.287 | convolution fusion | flops 1078984704 | bytes 9699328 | tf_op jit(solution)/shard_map/dot_general | solution.py:33
  271.9 5.2 %fusion.203 = f32[1024,256]{1,0:T(8,128)} fusion(f32[1024,256]{1,0:T(8,128)} %fusion.64, bf16[1024,1024]{0,1:T(8,128)(2,1)} %get-tuple-element.44, bf16[1024,1024]{0,1:T(8,128)(2,1)} %get-tuple-element.43, bf16[1024,256]{1,0:T(8,128)(2,1)} %get-tuple-element.111, bf16[1024,256]{1,0:T(8,128)(2,1)} %get-tuple-element.105), kind=kOutput, calls=%fused_computation.228 | convolution fusion | flops 1084489728 | bytes 7340032 | tf_op jit(solution)/shard_map/dot_general | solution.py:48
  304.4 4.6 %fusion.268 = f32[2048,1024]{0,1:T(8,128)} fusion(bf16[1024,128]{1,0:T(8,128)(2,1)S(1)} %get-tuple-element.83, bf16[1024,128]{1,0:T(8,128)(2,1)S(1)} %get-tuple-element.84, bf16[1024,128]{1,0:T(8,128)(2,1)S(1)} %fusion.454, bf16[1024,128]{1,0:T(8,128)(2,1)S(1)} %copy-done.9, bf16[1024,128]{1,0:T(8,128)(2,1)S(1)} %copy-done.8), kind=kOutput, calls=%fused_computation.295 | convolution fusion | flops 1078984704 | bytes 9699328 | tf_op jit(solution)/shard_map/dot_general | solution.py:33
  308.9 4.7 %fusion.272 = f32[2048,1024]{0,1:T(8,128)} fusion(bf16[1024,128]{1,0:T(8,128)(2,1)S(1)} %get-tuple-element.81, bf16[1024,128]{1,0:T(8,128)(2,1)S(1)} %get-tuple-element.82, bf16[1024,128]{1,0:T(8,128)(2,1)S(1)} %fusion.454, bf16[1024,128]{1,0:T(8,128)(2,1)S(1)} %copy-done.9, bf16[1024,128]{1,0:T(8,128)(2,1)S(1)} %copy-done.8), kind=kOutput, calls=%fused_computation.299 | convolution fusion | flops 1078984704 | bytes 9699328 | tf_op jit(solution)/shard_map/dot_general | solution.py:33
  313.6 4.6 %fusion.276 = f32[2048,1024]{0,1:T(8,128)} fusion(bf16[1024,128]{1,0:T(8,128)(2,1)S(1)} %get-tuple-element.80, bf16[1024,128]{1,0:T(8,128)(2,1)S(1)} %get-tuple-element.79, bf16[1024,128]{1,0:T(8,128)(2,1)S(1)} %fusion.454, bf16[1024,128]{1,0:T(8,128)(2,1)S(1)} %copy-done.9, bf16[1024,128]{1,0:T(8,128)(2,1)S(1)} %copy-done.8), kind=kOutput, calls=%fused_computation.303 | convolution fusion | flops 1078984704 | bytes 9699328 | tf_op jit(solution)/shard_map/dot_general | solution.py:33
  319.9 4.7 %fusion.296 = f32[2048,1024]{0,1:T(8,128)} fusion(bf16[1024,128]{1,0:T(8,128)(2,1)S(1)} %get-tuple-element.69, bf16[1024,128]{1,0:T(8,128)(2,1)S(1)} %get-tuple-element.70, bf16[1024,128]{1,0:T(8,128)(2,1)S(1)} %fusion.456, bf16[1024,128]{1,0:T(8,128)(2,1)S(1)} %copy-done.7, bf16[1024,128]{1,0:T(8,128)(2,1)S(1)} %get-tuple-element.118), kind=kOutput, calls=%fused_computation.323 | convolution fusion | flops 1078984704 | bytes 9699328 | tf_op jit(solution)/shard_map/dot_general | solution.py:33
  324.6 4.7 %fusion.300 = f32[2048,1024]{0,1:T(8,128)} fusion(bf16[1024,128]{1,0:T(8,128)(2,1)S(1)} %get-tuple-element.67, bf16[1024,128]{1,0:T(8,128)(2,1)S(1)} %get-tuple-element.68, bf16[1024,128]{1,0:T(8,128)(2,1)S(1)} %fusion.456, bf16[1024,128]{1,0:T(8,128)(2,1)S(1)} %copy-done.7, bf16[1024,128]{1,0:T(8,128)(2,1)S(1)} %get-tuple-element.118), kind=kOutput, calls=%fused_computation.327 | convolution fusion | flops 1078984704 | bytes 9699328 | tf_op jit(solution)/shard_map/dot_general | solution.py:33
  337.0 5.2 %fusion.191 = f32[1024,256]{1,0:T(8,128)} fusion(f32[1024,256]{1,0:T(8,128)} %fusion.80, bf16[1024,1024]{0,1:T(8,128)(2,1)} %get-tuple-element.36, bf16[1024,1024]{0,1:T(8,128)(2,1)} %get-tuple-element.35, bf16[1024,256]{1,0:T(8,128)(2,1)} %get-tuple-element.111, bf16[1024,256]{1,0:T(8,128)(2,1)} %get-tuple-element.105), kind=kOutput, calls=%fused_computation.224 | convolution fusion | flops 1084489728 | bytes 7340032 | tf_op jit(solution)/shard_map/dot_general | solution.py:48
  345.7 6.4 %fusion.15 = (bf16[1024,1024]{0,1:T(8,128)(2,1)}, bf16[1024,1024]{0,1:T(8,128)(2,1)}) fusion(f32[2048,1024]{0,1:T(8,128)} %fusion.296, bf16[6,4096,64]{1,2,0:T(8,128)(2,1)} %all-gather.11.cloned.1.call-done, bf16[6,1024,64]{1,2,0:T(8,128)(2,1)S(1)} %copy-done.3), kind=kOutput, calls=%fused_computation.31 | convolution fusion | flops 138412032 | bytes 12845056 | tf_op jit(solution)/shard_map/dot_general | solution.py:36
  393.2 7.3 %all-gather = f32[512,256]{1,0:T(8,128)S(1)} all-gather(f32[128,256]{1,0:T(8,128)S(1)} %fusion.220), channel_id=2, replica_groups=mesh['ka'=8,'pt'=4] {'pt'}, dimensions={0}, use_global_device_ids=true | all-gather | bytes 655360 | tf_op jit(solution)/shard_map/all_gather | solution.py:114
  (307 shorter events, 152.2 us)
Async XLA Ops:
  6.5 106.4 %copy-start = (bf16[48,128,128]{2,1,0:T(8,128)(2,1)S(1)}, bf16[48,128,128]{2,1,0:T(8,128)(2,1)}, u32[]{:S(2)}) copy-start(bf16[48,128,128]{2,1,0:T(8,128)(2,1)} %param.9) | copy-start | bytes 4718596
  11.1 7.5 %copy-start.63 = (s32[8,4]{0,1:T(4,128)S(1)}, s32[8,4]{0,1:T(4,128)}, u32[]{:S(2)}) copy-start(s32[8,4]{0,1:T(4,128)} %param.7) | copy-start | bytes 388
  11.1 7.5 %copy-start.64 = (s32[8,4]{0,1:T(4,128)S(1)}, s32[8,4]{0,1:T(4,128)}, u32[]{:S(2)}) copy-start(s32[8,4]{0,1:T(4,128)} %param.8) | copy-start | bytes 388
  11.1 100.7 %all-to-all-start = ((bf16[8,2,1024,128]{3,2,1,0:T(8,128)(2,1)}), bf16[8,2,1024,128]{3,2,1,0:T(8,128)(2,1)}, u32[]{:S(2)}, u32[]{:S(2)}) async-start(bf16[8,2,1024,128]{3,2,1,0:T(8,128)(2,1)} %broadcast_select_fusion), calls=%async_computation | async-start | bytes 8388608 | tf_op jit(solution)/shard_map/all_to_all | solution.py:77
  18.6 171.8 %all-gather.9.cloned.1.call-start = ((), (), s32[]{:S(2)}) async-start(), calls=%async_computation.1 | async-start | bytes 2621440 | tf_op jit(solution)/shard_map/all_gather | solution.py:81
  114.0 59.6 %copy-start.15 = (bf16[2048,128]{1,0:T(8,128)(2,1)S(1)}, bf16[2048,128]{1,0:T(8,128)(2,1)}, u32[]{:S(2)}) copy-start(bf16[2048,128]{1,0:T(8,128)(2,1)} %convolution_convert_fusion) | copy-start | bytes 1572868
  114.0 100.8 %all-gather.11.cloned.1.call-start = ((), (), s32[]{:S(2)}) async-start(), calls=%async_computation.2 | async-start | bytes 3932160 | tf_op jit(solution)/shard_map/all_gather | solution.py:82
  114.8 119.9 %all-gather.13.cloned.1.call-start = ((), (), s32[]{:S(2)}) async-start(), calls=%async_computation.3 | async-start | bytes 2621440 | tf_op jit(solution)/shard_map/all_gather | solution.py:94
  114.8 15.5 %collective-permute-start = (bf16[2,1024,128]{2,1,0:T(8,128)(2,1)}, bf16[2,1024,128]{2,1,0:T(8,128)(2,1)S(1)}, u32[]{:S(2)}, u32[]{:S(2)}) collective-permute-start(bf16[2,1024,128]{2,1,0:T(8,128)(2,1)} %bitcast.396), channel_id=1, source_target_pairs={{28,0},{0,4},{4,8},{8,12},{12,16},{16,20},{20,24},{24,28},{29,1},{... | collective-permute-start | bytes 1572872 | tf_op jit(solution)/shard_map/ppermute | solution.py:16
  131.2 42.5 %copy-start.25 = (bf16[2,1024,128]{2,1,0:T(8,128)(2,1)S(1)}, bf16[2,1024,128]{2,1,0:T(8,128)(2,1)}, u32[]{:S(2)}) copy-start(bf16[2,1024,128]{2,1,0:T(8,128)(2,1)} %copy-done.24) | copy-start | bytes 1572868
  131.2 124.5 %all-gather.17.cloned.1.call-start = ((), (), s32[]{:S(2)}) async-start(), calls=%async_computation.5 | async-start | bytes 2621440 | tf_op jit(solution)/shard_map/all_gather | solution.py:94
  131.2 12.0 %collective-permute-start.2 = (bf16[2,1024,128]{2,1,0:T(8,128)(2,1)}, bf16[2,1024,128]{2,1,0:T(8,128)(2,1)S(1)}, u32[]{:S(2)}, u32[]{:S(2)}) collective-permute-start(bf16[2,1024,128]{2,1,0:T(8,128)(2,1)} %bitcast.397), channel_id=1, source_target_pairs={{4,0},{8,4},{12,8},{16,12},{20,16},{24,20},{28,24},{0,28},{5,1},{9... | collective-permute-start | bytes 1572872 | tf_op jit(solution)/shard_map/ppermute | solution.py:16
  144.1 29.7 %copy-start.23 = (bf16[2,1024,128]{2,1,0:T(8,128)(2,1)S(1)}, bf16[2,1024,128]{2,1,0:T(8,128)(2,1)}, u32[]{:S(2)}) copy-start(bf16[2,1024,128]{2,1,0:T(8,128)(2,1)} %copy-done.22) | copy-start | bytes 1572868
  144.1 153.2 %all-gather.15.cloned.1.call-start = ((), (), s32[]{:S(2)}) async-start(), calls=%async_computation.4 | async-start | bytes 2621440 | tf_op jit(solution)/shard_map/all_gather | solution.py:94
  144.1 15.8 %collective-permute-start.1 = (bf16[2,1024,128]{2,1,0:T(8,128)(2,1)}, bf16[2,1024,128]{2,1,0:T(8,128)(2,1)S(1)}, u32[]{:S(2)}, u32[]{:S(2)}) collective-permute-start(bf16[2,1024,128]{2,1,0:T(8,128)(2,1)} %copy-done.24), channel_id=1, source_target_pairs={{28,0},{0,4},{4,8},{8,12},{12,16},{16,20},{20,24},{24,28},{29,1},{... | collective-permute-start | bytes 1572872 | tf_op jit(solution)/shard_map/ppermute | solution.py:16
  160.7 157.5 %all-gather.19.cloned.1.call-start = ((), (), s32[]{:S(2)}) async-start(), calls=%async_computation.6 | async-start | bytes 2621440 | tf_op jit(solution)/shard_map/all_gather | solution.py:94
  160.8 11.9 %collective-permute-start.3 = (bf16[2,1024,128]{2,1,0:T(8,128)(2,1)}, bf16[2,1024,128]{2,1,0:T(8,128)(2,1)S(1)}, u32[]{:S(2)}, u32[]{:S(2)}) collective-permute-start(bf16[2,1024,128]{2,1,0:T(8,128)(2,1)} %copy-done.22), channel_id=1, source_target_pairs={{4,0},{8,4},{12,8},{16,12},{20,16},{24,20},{28,24},{0,28},{5,1},{9... | collective-permute-start | bytes 1572872 | tf_op jit(solution)/shard_map/ppermute | solution.py:16
  173.5 199.7 %all-gather.21.cloned.1.call-start = ((), (), s32[]{:S(2)}) async-start(), calls=%async_computation.7 | async-start | bytes 2621440 | tf_op jit(solution)/shard_map/all_gather | solution.py:94
  176.3 12.4 %collective-permute-start.4 = (bf16[2,1024,128]{2,1,0:T(8,128)(2,1)S(1)}, bf16[2,1024,128]{2,1,0:T(8,128)(2,1)S(1)}, u32[]{:S(2)}, u32[]{:S(2)}) collective-permute-start(bf16[2,1024,128]{2,1,0:T(8,128)(2,1)S(1)} %copy-done.19), channel_id=1, source_target_pairs={{4,0},{8,4},{12,8},{16,12},{20,16},{24,20},{28,24},{0,28},{5,1},{9... | collective-permute-start | bytes 1572872 | tf_op jit(solution)/shard_map/ppermute | solution.py:16
  268.1 9.1 %slice-start.2 = ((s8[8388608]{0:T(1024)(128)(4,1)}), s8[4194304]{0:T(1024)(128)(4,1)S(1)}, s32[]{:S(2)}) async-start(s8[8388608]{0:T(1024)(128)(4,1)} %bitcast.377), calls=%async_computation.10 | async-start | bytes 8388608
  333.0 9.2 %slice-start.6 = ((s8[8388608]{0:T(1024)(128)(4,1)}), s8[4194304]{0:T(1024)(128)(4,1)S(1)}, s32[]{:S(2)}) async-start(s8[8388608]{0:T(1024)(128)(4,1)} %bitcast.381), calls=%async_computation.14 | async-start | bytes 8388608
  333.0 10.8 %slice-start.8 = ((s8[8388608]{0:T(1024)(128)(4,1)}), s8[4194304]{0:T(1024)(128)(4,1)S(1)}, s32[]{:S(2)}) async-start(s8[8388608]{0:T(1024)(128)(4,1)} %bitcast.383), calls=%async_computation.16 | async-start | bytes 8388608
  343.9 8.3 %slice-start.14 = ((s8[8388608]{0:T(1024)(128)(4,1)}), s8[4194304]{0:T(1024)(128)(4,1)S(1)}, s32[]{:S(2)}) async-start(s8[8388608]{0:T(1024)(128)(4,1)} %bitcast.389), calls=%async_computation.22 | async-start | bytes 8388608
  392.8 8.4 %copy-start.1 = (bf16[48,128,128]{2,1,0:T(8,128)(2,1)S(1)}, bf16[48,128,128]{2,1,0:T(8,128)(2,1)}, u32[]{:S(2)}) copy-start(bf16[48,128,128]{2,1,0:T(8,128)(2,1)} %param.9) | copy-start | bytes 4718596
  (80 other events, 186.0 us)
Sparse Core Ops, SparseCore 0:
  114.2 21.6 all-gather.8
  137.4 28.4 all-gather.10
  167.5 22.5 all-gather.12
  191.5 22.5 all-gather.16
  215.5 22.5 all-gather.14
  239.5 22.5 all-gather.18
  263.7 22.5 all-gather.20
